TPU v7x, 128 devices: a whole 4x4x4 slice. The times are simulated.
128 devices in a mesh: ha: 16 (over z, y_lo, core), wa: 8 (over x, y_hi).
Axes of the slice: x: 4, y: 4 (y_hi: 2, y_lo: 2; y = y_hi * 2 + y_lo), z: 4, core: 2. Of those that a mesh axis runs over, the one named last changes fastest.
Arguments:
- tokens: bfloat16 [256, 256, 512], P('ha', 'wa'), may hold values from -40 to 40
- cotangent: bfloat16 [256, 256, 512], P('ha', 'wa'), may hold values from -6 to 6
- norm_gain: float32 [512], replicated, may hold values from 0.1 to 1.9
- in_weight: bfloat16 [512, 1536], replicated, may hold values from -0.25 to 0.25
- out_weight: bfloat16 [512, 512], replicated, may hold values from -0.25 to 0.25
- bias_table: float32 [16, 31, 31], replicated, may hold values from -256 to 256
Outputs:
- grad_input: bfloat16 [256, 256, 512], P('ha', 'wa')
- grad_table: float32 [16, 31, 31], replicated
All inputs are finite; a program needn't handle non-finite values.
Results may differ from a plain program's by a relative error of at most 0.011.
Values may be sent and summed in bfloat16 or wider, within the bound.
No kernel may reach another device: no remote copies, remote signals or barrier semaphores. Data moves between devices by JAX's collectives and lax.ppermute only.
A program may use at most 128 MiB of HBM per device.

v0:
```python
import jax
import jax.numpy as jnp
from jax import lax
from jax.sharding import PartitionSpec as P

D = 512
HEADS = 16
HEAD_DIM = 32
WIN = 16
TAB = 31
NORM_EPS = 1e-05


def offset_hot():
    places = jnp.arange(WIN)
    slot_ids = jnp.arange(TAB)
    return (
        places[:, None, None] - places[None, :, None] + (WIN - 1) == slot_ids[None, None, :]
    ).astype(jnp.float32)


def full_bias(bias_table, offset_table):
    partial_rows = jnp.einsum(
        "abd,hde->habe", offset_table, bias_table, precision=lax.Precision.HIGHEST
    )
    spread = jnp.einsum(
        "uve,habe->haubv", offset_table, partial_rows, precision=lax.Precision.HIGHEST
    )
    return spread.reshape(HEADS, WIN * WIN, WIN * WIN)


def group_grad(group_tokens, group_cot, norm_gain, in_weight, out_weight, bias_full, offset_table):
    group_rows = WIN * WIN
    tokens_wide = group_tokens.astype(jnp.float32)
    center = jnp.mean(tokens_wide, axis=-1, keepdims=True)
    shifted = tokens_wide - center
    inv_std = lax.rsqrt(jnp.mean(shifted * shifted, axis=-1, keepdims=True) + NORM_EPS)
    unit_rows = shifted * inv_std
    normed = (unit_rows * norm_gain).astype(jnp.bfloat16)
    mixed_rows = jnp.dot(normed, in_weight, preferred_element_type=jnp.float32)
    query_scale = HEAD_DIM ** (-0.5)
    queries = (
        (mixed_rows[:, :D] * query_scale).astype(jnp.bfloat16).reshape(group_rows, HEADS, HEAD_DIM)
    )
    key_rows = mixed_rows[:, D : 2 * D].astype(jnp.bfloat16).reshape(group_rows, HEADS, HEAD_DIM)
    values = mixed_rows[:, 2 * D :].astype(jnp.bfloat16).reshape(group_rows, HEADS, HEAD_DIM)
    scores = (
        jnp.einsum("thd,shd->hts", queries, key_rows, preferred_element_type=jnp.float32)
        + bias_full
    )
    row_top = jnp.max(scores, axis=-1, keepdims=True)
    exponent = jnp.exp(scores - row_top)
    attn_probs = exponent / jnp.sum(exponent, axis=-1, keepdims=True)
    probs_half = attn_probs.astype(jnp.bfloat16)
    grad_out = lax.dot_general(
        group_cot, out_weight, (((1,), (1,)), ((), ())), preferred_element_type=jnp.float32
    )
    grad_out = grad_out.astype(jnp.bfloat16).reshape(group_rows, HEADS, HEAD_DIM)
    grad_probs = jnp.einsum("thd,shd->hts", grad_out, values, preferred_element_type=jnp.float32)
    grad_values = jnp.einsum(
        "hts,thd->shd", probs_half, grad_out, preferred_element_type=jnp.float32
    ).astype(jnp.bfloat16)
    grad_scores = attn_probs * (
        grad_probs - jnp.sum(attn_probs * grad_probs, axis=-1, keepdims=True)
    )
    scores_half = grad_scores.astype(jnp.bfloat16)
    grad_queries = (
        jnp.einsum("hts,shd->thd", scores_half, key_rows, preferred_element_type=jnp.float32)
        * query_scale
    ).astype(jnp.bfloat16)
    grad_keys = jnp.einsum(
        "hts,thd->shd", scores_half, queries, preferred_element_type=jnp.float32
    ).astype(jnp.bfloat16)
    grad_mixed = jnp.concatenate(
        [
            grad_queries.reshape(group_rows, D),
            grad_keys.reshape(group_rows, D),
            grad_values.reshape(group_rows, D),
        ],
        axis=1,
    )
    grad_normed = lax.dot_general(
        grad_mixed, in_weight, (((1,), (1,)), ((), ())), preferred_element_type=jnp.float32
    )
    grad_unit = grad_normed * norm_gain
    grad_rows = inv_std * (
        grad_unit
        - jnp.mean(grad_unit, axis=-1, keepdims=True)
        - unit_rows * jnp.mean(grad_unit * unit_rows, axis=-1, keepdims=True)
    )
    folded = jnp.einsum(
        "haubv,uve->habe",
        grad_scores.reshape(HEADS, WIN, WIN, WIN, WIN),
        offset_table,
        precision=lax.Precision.HIGHEST,
    )
    table_part = jnp.einsum("habe,abd->hde", folded, offset_table, precision=lax.Precision.HIGHEST)
    return (grad_rows.astype(jnp.bfloat16), table_part)


def body(tokens, cotangent, norm_gain, in_weight, out_weight, bias_table):
    offset_table = offset_hot()
    bias_full = full_bias(bias_table, offset_table)
    high_parts = lax.axis_size("ha")
    wide_parts = lax.axis_size("wa")
    rows_local, cols_local, channels = tokens.shape
    row_steps = WIN // high_parts
    col_steps = WIN // wide_parts
    stride_h = rows_local // row_steps
    stride_w = cols_local // col_steps
    row_groups = stride_h // high_parts
    col_groups = stride_w // wide_parts
    group_count = row_groups * col_groups

    def to_layout(tile_block):
        laid = tile_block.reshape(
            row_steps, high_parts, row_groups, col_steps, wide_parts, col_groups, channels
        )
        laid = laid.transpose(2, 5, 1, 4, 0, 3, 6)
        return laid.reshape(group_count, high_parts, wide_parts, row_steps, col_steps, channels)

    def one_group(pair_rows):
        return group_grad(
            pair_rows[0], pair_rows[1], norm_gain, in_weight, out_weight, bias_full, offset_table
        )

    laid_tokens = to_layout(tokens)
    laid_cot = to_layout(cotangent)

    def swap_rows(laid):
        items = laid.shape[0]
        shaped = laid.reshape(items, high_parts, wide_parts, row_steps, col_steps, channels)
        return shaped.transpose(0, 1, 3, 2, 4, 5).reshape(items, WIN * WIN, channels)

    flat_shape = (group_count, high_parts * wide_parts, row_steps * col_steps, channels)
    grad_rows, table_parts = lax.map(
        one_group,
        (
            swap_rows(
                lax.all_to_all(
                    laid_tokens.reshape(flat_shape),
                    ("ha", "wa"),
                    split_axis=1,
                    concat_axis=1,
                    tiled=True,
                )
            ),
            swap_rows(
                lax.all_to_all(
                    laid_cot.reshape(flat_shape),
                    ("ha", "wa"),
                    split_axis=1,
                    concat_axis=1,
                    tiled=True,
                )
            ),
        ),
    )
    items = grad_rows.shape[0]
    shaped = grad_rows.reshape(items, high_parts, row_steps, wide_parts, col_steps, channels)
    grads_laid, table_parts = (
        shaped.transpose(0, 1, 3, 2, 4, 5).reshape(
            items, high_parts * wide_parts, row_steps * col_steps, channels
        ),
        table_parts,
    )
    returned = lax.all_to_all(grads_laid, ("ha", "wa"), split_axis=1, concat_axis=1, tiled=True)
    returned = returned.reshape(group_count, high_parts, wide_parts, row_steps, col_steps, channels)
    shaped = returned.reshape(
        row_groups, col_groups, high_parts, wide_parts, row_steps, col_steps, channels
    )
    shaped = shaped.transpose(4, 2, 0, 5, 3, 1, 6)
    grad_input = shaped.reshape(rows_local, cols_local, channels)
    grad_table = lax.psum(jnp.sum(table_parts, axis=0), ("ha", "wa"))
    return (grad_input, grad_table)


def solution(mesh):
    in_specs = (P("ha", "wa", None), P("ha", "wa", None), P(), P(), P(), P())
    out_specs = (P("ha", "wa", None), P())
    return jax.shard_map(body, mesh=mesh, in_specs=in_specs, out_specs=out_specs, check_vma=False)
```

profile of v0, /device:TPU:1, one launch (start us, length us, event | category | flops | bytes accessed | tf_op | source)
XLA Modules:
  0.0 330.3 jit_solution(11427729656623690947)
XLA Ops:
  0.6 1.3 reshape.82
  1.9 1.6 copy.72
  3.5 11.5 %all-to-all-start = ((bf16[2,128,2,512]{3,2,0,1:T(2,128)(2,1)}), bf16[2,128,2,512]{3,2,0,1:T(2,128)(2,1)S(1)}, u32[]{:S(2)}, u32[]{:S(2)}) async-start(bf16[2,128,2,512]{3,2,0,1:T(2,128)(2,1)} %bitcast.1), calls=%async_computation | async-start | bytes 1048576 | tf_op jit(solution)/shard_map/all_to_all | solution.py:140
  15.7 1.2 reshape.84
  17.0 1.6 copy.76
  19.6 9.5 %all-to-all-done = bf16[2,128,2,512]{3,2,0,1:T(2,128)(2,1)S(1)} async-done(((bf16[2,128,2,512]{3,2,0,1:T(2,128)(2,1)}), bf16[2,128,2,512]{3,2,0,1:T(2,128)(2,1)S(1)}, u32[]{:S(2)}, u32[]{:S(2)}) %all-to-all-start) | async-done | bytes 524320 | tf_op jit(solution)/shard_map/all_to_all | solution.py:140
  29.1 4.7 %all-to-all-start.1 = ((bf16[2,128,2,512]{3,2,0,1:T(2,128)(2,1)}), bf16[2,128,2,512]{3,2,0,1:T(2,128)(2,1)}, u32[]{:S(2)}, u32[]{:S(2)}) async-start(bf16[2,128,2,512]{3,2,0,1:T(2,128)(2,1)} %bitcast.12), calls=%async_computation.1 | async-start | bytes 1048576 | tf_op jit(solution)/shard_map/all_to_all | solution.py:149
  33.8 17.4 %convolution_bitcast_fusion = f32[16,16,16,16,16]{4,3,2,1,0:T(8,128)} fusion(f32[16,16,16,31]{3,1,0,2:T(8,128)S(1)} %fusion.54, s32[16,16]{1,0:T(8,128)S(1)} %copy.74), kind=kOutput, calls=%fused_computation.64 | convolution fusion | flops 390078208 | bytes 4703232 | tf_op jit(solution)/shard_map/uve,habe->haubv/dot_general | solution.py:26
  51.2 23.5 %reshape.83 = f32[16,256,256]{2,1,0:T(8,128)} reshape(f32[16,16,16,16,16]{4,3,2,1,0:T(8,128)} %convolution_bitcast_fusion) | data formatting | bytes 8388608 | tf_op jit(solution)/shard_map/reshape | solution.py:29
  74.7 5.4 %copy.79 = f32[16,256,256]{1,2,0:T(8,128)} copy(f32[16,256,256]{2,1,0:T(8,128)} %reshape.83) | data formatting | bytes 8388608
  80.7 1.6 copy.77
  83.1 162.9 %while.14 = (s32[]{:T(128)}, bf16[2,256,512]{2,1,0:T(8,128)(2,1)}, f32[2,16,31,31]{2,3,1,0:T(8,128)}, bf16[2,256,512]{2,1,0:T(8,128)(2,1)S(1)}, f32[512]{0:T(512...) while((s32[]{:T(128)}, bf16[2,256,512]{2,1,0:T(8,128)(2,1)}, ...), condition=%wide.region_8.9_spmd.clone.clone, body=%wide.region_0.8_spmd.clone.clone.sunk | while | flops 1734164224 | bytes 137940368 | solution.py:136
  83.7 1.3 convolution_convert_fusion.4
  91.3 2.9 convolution_add_fusion.2
  94.3 3.1 fusion.130
  97.5 5.2 %fusion.131 = bf16[16,32,256]{2,1,0:T(8,128)(2,1)} fusion(bf16[256,16,32]{0,2,1:T(8,128)(2,1)S(1)} %bitcast.193, f32[16,256]{1,0:T(8,128)S(1)} %get-tuple-element.273, f32[16,256,256]{1,2,0:T(8,128)} %copy-done.4), kind=kOutput, calls=%fused_computation.13.clone.1 | convolution fusion | flops 70390016 | bytes 4734976 | tf_op jit(solution)/shard_map/while/body/eval_jaxpr/hts,thd->shd/dot_general | solution.py:60
  102.7 3.2 multiply_reduce_fusion.2
  110.5 19.4 %reshape.111 = f32[16,16,16,16,16]{2,1,4,3,0:T(8,128)} reshape(f32[16,256,256]{1,2,0:T(8,128)} %copy-done.2) | data formatting | bytes 8388608 | tf_op jit(solution)/shard_map/while/body/eval_jaxpr/reshape | solution.py:93
  129.9 30.4 %fusion.135 = f32[16,16,16,31,1]{3,1,4,2,0:T(8,128)S(1)} fusion(f32[16,16,16,16,16]{2,1,4,3,0:T(8,128)} %reshape.111, s32[16,16]{0,1:T(8,128)S(1)} %get-tuple-element.314), kind=kOutput, calls=%fused_computation.53.clone.1 | convolution fusion | flops 390086144 | bytes 4703232 | tf_op jit(solution)/shard_map/while/body/eval_jaxpr/haubv,uve->habe/dot_general | solution.py:91
  160.4 3.5 %fusion.136 = f32[2,16,31,31]{2,3,1,0:T(8,128)S(1)} fusion(f32[2,16,31,31]{2,3,1,0:T(8,128)S(1)} %copy-done.13, s32[]{:T(128)S(6)} %copy.114, f32[16,16,16,31,1]{3,1,4,2,0:T(8,128)S(1)} %fusion.135, s32[16,16]{0,1:T(8,128)S(1)} %get-tuple-element.314), kind=kOutput, calls=%fused_computation.18.clone.1 | convolution fusion | flops 47250944 | bytes 2367492 | tf_op jit(solution)/shard_map/while/body/eval_jaxpr/habe,abd->hde/dot_general | solution.py:97
  165.0 1.3 convolution_convert_fusion.4
  172.7 2.9 convolution_add_fusion.2
  175.6 3.1 fusion.130
  178.8 5.2 %fusion.131 = bf16[16,32,256]{2,1,0:T(8,128)(2,1)} fusion(bf16[256,16,32]{0,2,1:T(8,128)(2,1)S(1)} %bitcast.193, f32[16,256]{1,0:T(8,128)S(1)} %get-tuple-element.273, f32[16,256,256]{1,2,0:T(8,128)} %copy-done.4), kind=kOutput, calls=%fused_computation.13.clone.1 | convolution fusion | flops 70390016 | bytes 4734976 | tf_op jit(solution)/shard_map/while/body/eval_jaxpr/hts,thd->shd/dot_general | solution.py:60
  184.0 3.2 multiply_reduce_fusion.2
  191.9 19.4 %reshape.111 = f32[16,16,16,16,16]{2,1,4,3,0:T(8,128)} reshape(f32[16,256,256]{1,2,0:T(8,128)} %copy-done.2) | data formatting | bytes 8388608 | tf_op jit(solution)/shard_map/while/body/eval_jaxpr/reshape | solution.py:93
  211.3 30.4 %fusion.135 = f32[16,16,16,31,1]{3,1,4,2,0:T(8,128)S(1)} fusion(f32[16,16,16,16,16]{2,1,4,3,0:T(8,128)} %reshape.111, s32[16,16]{0,1:T(8,128)S(1)} %get-tuple-element.314), kind=kOutput, calls=%fused_computation.53.clone.1 | convolution fusion | flops 390086144 | bytes 4703232 | tf_op jit(solution)/shard_map/while/body/eval_jaxpr/haubv,uve->habe/dot_general | solution.py:91
  241.7 3.5 %fusion.136 = f32[2,16,31,31]{2,3,1,0:T(8,128)S(1)} fusion(f32[2,16,31,31]{2,3,1,0:T(8,128)S(1)} %copy-done.13, s32[]{:T(128)S(6)} %copy.114, f32[16,16,16,31,1]{3,1,4,2,0:T(8,128)S(1)} %fusion.135, s32[16,16]{0,1:T(8,128)S(1)} %get-tuple-element.314), kind=kOutput, calls=%fused_computation.18.clone.1 | convolution fusion | flops 47250944 | bytes 2367492 | tf_op jit(solution)/shard_map/while/body/eval_jaxpr/habe,abd->hde/dot_general | solution.py:97
  246.0 2.4 copy.81
  248.4 9.9 %all-to-all-start.2 = ((bf16[2,128,2,512]{3,0,2,1:T(2,128)(2,1)}), bf16[2,128,2,512]{3,0,2,1:T(2,128)(2,1)S(1)}, u32[]{:S(2)}, u32[]{:S(2)}) async-start(bf16[2,128,2,512]{3,0,2,1:T(2,128)(2,1)} %bitcast.14), calls=%async_computation.2 | async-start | bytes 1048576 | tf_op jit(solution)/shard_map/all_to_all | solution.py:167
  258.3 1.1 reduce_sum.63
  259.4 68.6 %psum.7 = f32[16,31,31]{1,2,0:T(8,128)S(1)} all-reduce(f32[16,31,31]{1,2,0:T(8,128)S(1)} %reduce_sum.63), channel_id=1, replica_groups=mesh['ha'=16,'wa'=8] {'ha','wa'}, use_global_device_ids=true, to_apply=%region_10.11 | all-reduce | flops 15376 | bytes 123008 | tf_op jit(solution)/shard_map/psum | solution.py:174
  (98 shorter events, 29.8 us)
Async XLA Ops:
  0.6 18.0 %copy-start = (f32[16,31,31]{2,0,1:T(8,128)S(1)}, f32[16,31,31]{2,0,1:T(8,128)}, u32[]{:S(2)}) copy-start(f32[16,31,31]{2,0,1:T(8,128)} %param.13) | copy-start | bytes 184516
  3.5 25.5 %all-to-all-start = ((bf16[2,128,2,512]{3,2,0,1:T(2,128)(2,1)}), bf16[2,128,2,512]{3,2,0,1:T(2,128)(2,1)S(1)}, u32[]{:S(2)}, u32[]{:S(2)}) async-start(bf16[2,128,2,512]{3,2,0,1:T(2,128)(2,1)} %bitcast.1), calls=%async_computation | async-start | bytes 1048576 | tf_op jit(solution)/shard_map/all_to_all | solution.py:140
  15.0 0.6 copy-start.11
  29.1 22.1 %copy-start.9 = (bf16[2,128,2,512]{3,2,0,1:T(2,128)(2,1)}, bf16[2,128,2,512]{3,2,0,1:T(2,128)(2,1)S(1)}, u32[]{:S(2)}) copy-start(bf16[2,128,2,512]{3,2,0,1:T(2,128)(2,1)S(1)} %all-to-all-done) | copy-start | bytes 1572868
  29.1 51.6 %all-to-all-start.1 = ((bf16[2,128,2,512]{3,2,0,1:T(2,128)(2,1)}), bf16[2,128,2,512]{3,2,0,1:T(2,128)(2,1)}, u32[]{:S(2)}, u32[]{:S(2)}) async-start(bf16[2,128,2,512]{3,2,0,1:T(2,128)(2,1)} %bitcast.12), calls=%async_computation.1 | async-start | bytes 1048576 | tf_op jit(solution)/shard_map/all_to_all | solution.py:149
  74.7 5.4 %copy-start.10 = (bf16[2,128,2,512]{3,2,0,1:T(2,128)(2,1)S(1)}, bf16[2,128,2,512]{3,2,0,1:T(2,128)(2,1)}, u32[]{:S(2)}) copy-start(bf16[2,128,2,512]{3,2,0,1:T(2,128)(2,1)} %copy-done.9) | copy-start | bytes 1572868
  80.1 3.0 copy-start.5
  80.1 3.0 copy-start.6
  80.2 3.0 copy-start.12
  80.2 3.0 copy-start.15
  94.3 3.2 copy-start.4
  94.3 3.2 copy-start.8
  102.7 3.4 %copy-start.3 = (f32[16,256,256]{1,2,0:T(8,128)S(1)}, f32[16,256,256]{1,2,0:T(8,128)}, u32[]{:S(2)}) copy-start(f32[16,256,256]{1,2,0:T(8,128)} %get-tuple-element.274) | copy-start | bytes 12582916 | tf_op jit(solution)/shard_map/while
  106.9 2.0 copy-start.2
  106.9 2.0 copy-start.16
  129.9 30.4 %copy-start.13 = (f32[2,16,31,31]{2,3,1,0:T(8,128)S(1)}, f32[2,16,31,31]{2,3,1,0:T(8,128)}, u32[]{:S(2)}) copy-start(f32[2,16,31,31]{2,3,1,0:T(8,128)} %get-tuple-element.296) | copy-start | bytes 369028 | tf_op jit(solution)/shard_map/while
  129.9 34.7 %copy-start.7 = (bf16[512,512]{1,0:T(8,128)(2,1)S(1)}, bf16[512,512]{1,0:T(8,128)(2,1)}, u32[]{:S(2)}) copy-start(bf16[512,512]{1,0:T(8,128)(2,1)} %get-tuple-element.327) | copy-start | bytes 1572868 | tf_op jit(solution)/shard_map/while
  163.9 0.8 copy-start.14
  175.6 3.2 copy-start.4
  175.6 3.2 copy-start.8
  184.0 3.4 %copy-start.3 = (f32[16,256,256]{1,2,0:T(8,128)S(1)}, f32[16,256,256]{1,2,0:T(8,128)}, u32[]{:S(2)}) copy-start(f32[16,256,256]{1,2,0:T(8,128)} %get-tuple-element.274) | copy-start | bytes 12582916 | tf_op jit(solution)/shard_map/while
  188.2 2.0 copy-start.2
  188.2 2.0 copy-start.16
  211.3 30.4 %copy-start.13 = (f32[2,16,31,31]{2,3,1,0:T(8,128)S(1)}, f32[2,16,31,31]{2,3,1,0:T(8,128)}, u32[]{:S(2)}) copy-start(f32[2,16,31,31]{2,3,1,0:T(8,128)} %get-tuple-element.296) | copy-start | bytes 369028 | tf_op jit(solution)/shard_map/while
  211.3 34.7 %copy-start.7 = (bf16[512,512]{1,0:T(8,128)(2,1)S(1)}, bf16[512,512]{1,0:T(8,128)(2,1)}, u32[]{:S(2)}) copy-start(bf16[512,512]{1,0:T(8,128)(2,1)} %get-tuple-element.327) | copy-start | bytes 1572868 | tf_op jit(solution)/shard_map/while
  245.2 0.8 copy-start.14
  246.0 84.3 %copy-start.1 = (f32[16,31,31]{2,0,1:T(8,128)S(1)}, f32[16,31,31]{2,0,1:T(8,128)}, u32[]{:S(2)}) copy-start(f32[16,31,31]{2,0,1:T(8,128)} %param.13) | copy-start | bytes 184516
  248.4 80.5 %all-to-all-start.2 = ((bf16[2,128,2,512]{3,0,2,1:T(2,128)(2,1)}), bf16[2,128,2,512]{3,0,2,1:T(2,128)(2,1)S(1)}, u32[]{:S(2)}, u32[]{:S(2)}) async-start(bf16[2,128,2,512]{3,0,2,1:T(2,128)(2,1)} %bitcast.14), calls=%async_computation.2 | async-start | bytes 1048576 | tf_op jit(solution)/shard_map/all_to_all | solution.py:167
where the time goes:
time: 332 us; the launch traced here: 330 us
  matrix products  117 us (35%)
  local copies, waits for them, and re-layouts  95.5 us (29%)
  blocking collectives  68.6 us (21%)
  starting transfers between devices  26.1 us (8%)
  other arithmetic  12.9 us (4%)
  waiting for transfers between devices  9.46 us (3%)
    psum x1, blocking collectives, body(): grad_table = lax.psum(jnp.sum(table_parts, axis=0), ('ha', 'wa'))  68.6 us
    dot_general x2, matrix products, group_grad(): jnp.einsum('haubv,uve->habe', grad_scores.reshape(HEADS, WIN, WIN, WIN, W...  60.8 us
    reshape x2, local copies, waits for them, and re-layouts, group_grad(): grad_scores.reshape(HEADS, WIN, WIN, WIN, WIN)  38.8 us
    reshape x1, local copies, waits for them, and re-layouts, full_bias(): return spread.reshape(HEADS, WIN * WIN, WIN * WIN)  23.5 us
    dot_general x1, matrix products, full_bias(): jnp.einsum('uve,habe->haubv', offset_table, partial_rows, precision=lax.P...  17.4 us
    all_to_all x1, starting transfers between devices, body(): lax.all_to_all(laid_tokens.reshape(flat_shape), ('ha', 'wa'), split_axis=...  11.5 us
    dot_general x2, matrix products, group_grad(): jnp.einsum('hts,thd->shd', probs_half, grad_out, preferred_element_type=j...  10.3 us
    all_to_all x1, starting transfers between devices, body(): lax.all_to_all(grads_laid, ('ha', 'wa'), split_axis=1, concat_axis=1, til...  9.89 us
  transfers between devices with their start and end apart: 3, of which 1 were waited for; matrix products, arithmetic and copies ran while one was open for 16% of the time, Pallas kernels for 0%

commit v1 on v0

--- a/solution.py
+++ b/solution.py
@@ -171,7 +171,7 @@
     )
     shaped = shaped.transpose(4, 2, 0, 5, 3, 1, 6)
     grad_input = shaped.reshape(rows_local, cols_local, channels)
-    grad_table = lax.psum(jnp.sum(table_parts, axis=0), ("ha", "wa"))
+    grad_table = lax.psum(lax.psum(jnp.sum(table_parts, axis=0), "ha"), "wa")
     return (grad_input, grad_table)
 
 

time: 332 us -> 367 us (1.11)
  the two profiles are of different devices: /device:TPU:1 before, /device:TPU:0 now
where the time goes in v1:
time: 367 us; the launch traced here: 365 us
  matrix products  116 us (32%)
  blocking collectives  103 us (28%)
  local copies, waits for them, and re-layouts  95.4 us (26%)
  starting transfers between devices  26.6 us (7%)
  other arithmetic  12.9 us (4%)
  waiting for transfers between devices  8.62 us (2%)
    psum x2, blocking collectives, body(): grad_table = lax.psum(lax.psum(jnp.sum(table_parts, axis=0), 'ha'), 'wa')  103 us
    dot_general x2, matrix products, group_grad(): jnp.einsum('haubv,uve->habe', grad_scores.reshape(HEADS, WIN, WIN, WIN, W...  60.8 us
    reshape x2, local copies, waits for them, and re-layouts, group_grad(): grad_scores.reshape(HEADS, WIN, WIN, WIN, WIN)  38.8 us
    reshape x1, local copies, waits for them, and re-layouts, full_bias(): return spread.reshape(HEADS, WIN * WIN, WIN * WIN)  23.5 us
    dot_general x1, matrix products, full_bias(): jnp.einsum('uve,habe->haubv', offset_table, partial_rows, precision=lax.P...  17.4 us
    all_to_all x1, starting transfers between devices, body(): lax.all_to_all(laid_tokens.reshape(flat_shape), ('ha', 'wa'), split_axis=...  11.2 us
    dot_general x2, matrix products, group_grad(): jnp.einsum('hts,thd->shd', probs_half, grad_out, preferred_element_type=j...  10.3 us
    all_to_all x1, starting transfers between devices, body(): lax.all_to_all(grads_laid, ('ha', 'wa'), split_axis=1, concat_axis=1, til...  9.69 us
  transfers between devices with their start and end apart: 3, of which 1 were waited for; matrix products, arithmetic and copies ran while one was open for 14% of the time, Pallas kernels for 0%

profile of v1, /device:TPU:0, one launch (start us, length us, event | category | flops | bytes accessed | tf_op | source)
XLA Modules:
  0.0 364.7 jit_solution(2962486937305774323)
XLA Ops:
  0.6 1.3 reshape.82
  1.9 1.6 copy.72
  3.5 11.2 %all-to-all-start = ((bf16[2,128,2,512]{3,2,0,1:T(2,128)(2,1)}), bf16[2,128,2,512]{3,2,0,1:T(2,128)(2,1)S(1)}, u32[]{:S(2)}, u32[]{:S(2)}) async-start(bf16[2,128,2,512]{3,2,0,1:T(2,128)(2,1)} %bitcast.1), calls=%async_computation | async-start | bytes 1048576 | tf_op jit(solution)/shard_map/all_to_all | solution.py:140
  15.4 1.2 reshape.84
  16.6 1.6 copy.76
  19.3 8.6 %all-to-all-done = bf16[2,128,2,512]{3,2,0,1:T(2,128)(2,1)S(1)} async-done(((bf16[2,128,2,512]{3,2,0,1:T(2,128)(2,1)}), bf16[2,128,2,512]{3,2,0,1:T(2,128)(2,1)S(1)}, u32[]{:S(2)}, u32[]{:S(2)}) %all-to-all-start) | async-done | bytes 524320 | tf_op jit(solution)/shard_map/all_to_all | solution.py:140
  27.9 5.7 %all-to-all-start.1 = ((bf16[2,128,2,512]{3,2,0,1:T(2,128)(2,1)}), bf16[2,128,2,512]{3,2,0,1:T(2,128)(2,1)}, u32[]{:S(2)}, u32[]{:S(2)}) async-start(bf16[2,128,2,512]{3,2,0,1:T(2,128)(2,1)} %bitcast.12), calls=%async_computation.1 | async-start | bytes 1048576 | tf_op jit(solution)/shard_map/all_to_all | solution.py:149
  33.7 17.4 %convolution_bitcast_fusion = f32[16,16,16,16,16]{4,3,2,1,0:T(8,128)} fusion(f32[16,16,16,31]{3,1,0,2:T(8,128)S(1)} %fusion.54, s32[16,16]{1,0:T(8,128)S(1)} %copy.74), kind=kOutput, calls=%fused_computation.64 | convolution fusion | flops 390078208 | bytes 4703232 | tf_op jit(solution)/shard_map/uve,habe->haubv/dot_general | solution.py:26
  51.1 23.5 %reshape.83 = f32[16,256,256]{2,1,0:T(8,128)} reshape(f32[16,16,16,16,16]{4,3,2,1,0:T(8,128)} %convolution_bitcast_fusion) | data formatting | bytes 8388608 | tf_op jit(solution)/shard_map/reshape | solution.py:29
  74.6 5.4 %copy.79 = f32[16,256,256]{1,2,0:T(8,128)} copy(f32[16,256,256]{2,1,0:T(8,128)} %reshape.83) | data formatting | bytes 8388608
  80.6 1.6 copy.77
  83.0 162.7 %while.14 = (s32[]{:T(128)}, bf16[2,256,512]{2,1,0:T(8,128)(2,1)}, f32[2,16,31,31]{2,3,1,0:T(8,128)}, bf16[2,256,512]{2,1,0:T(8,128)(2,1)S(1)}, f32[512]{0:T(512...) while((s32[]{:T(128)}, bf16[2,256,512]{2,1,0:T(8,128)(2,1)}, ...), condition=%wide.region_8.9_spmd.clone.clone, body=%wide.region_0.8_spmd.clone.clone.sunk | while | flops 1734164224 | bytes 137940368 | solution.py:136
  83.6 1.3 convolution_convert_fusion.4
  91.2 2.9 convolution_add_fusion.2
  94.2 3.1 fusion.130
  97.3 5.1 %fusion.131 = bf16[16,32,256]{2,1,0:T(8,128)(2,1)} fusion(bf16[256,16,32]{0,2,1:T(8,128)(2,1)S(1)} %bitcast.193, f32[16,256]{1,0:T(8,128)S(1)} %get-tuple-element.273, f32[16,256,256]{1,2,0:T(8,128)} %copy-done.4), kind=kOutput, calls=%fused_computation.13.clone.1 | convolution fusion | flops 70390016 | bytes 4734976 | tf_op jit(solution)/shard_map/while/body/eval_jaxpr/hts,thd->shd/dot_general | solution.py:60
  102.5 3.2 multiply_reduce_fusion.2
  110.3 19.4 %reshape.111 = f32[16,16,16,16,16]{2,1,4,3,0:T(8,128)} reshape(f32[16,256,256]{1,2,0:T(8,128)} %copy-done.2) | data formatting | bytes 8388608 | tf_op jit(solution)/shard_map/while/body/eval_jaxpr/reshape | solution.py:93
  129.8 30.4 %fusion.135 = f32[16,16,16,31,1]{3,1,4,2,0:T(8,128)S(1)} fusion(f32[16,16,16,16,16]{2,1,4,3,0:T(8,128)} %reshape.111, s32[16,16]{0,1:T(8,128)S(1)} %get-tuple-element.314), kind=kOutput, calls=%fused_computation.53.clone.1 | convolution fusion | flops 390086144 | bytes 4703232 | tf_op jit(solution)/shard_map/while/body/eval_jaxpr/haubv,uve->habe/dot_general | solution.py:91
  160.2 3.5 fusion.136
  164.9 1.3 convolution_convert_fusion.4
  172.5 2.9 convolution_add_fusion.2
  175.4 3.1 fusion.130
  178.6 5.1 %fusion.131 = bf16[16,32,256]{2,1,0:T(8,128)(2,1)} fusion(bf16[256,16,32]{0,2,1:T(8,128)(2,1)S(1)} %bitcast.193, f32[16,256]{1,0:T(8,128)S(1)} %get-tuple-element.273, f32[16,256,256]{1,2,0:T(8,128)} %copy-done.4), kind=kOutput, calls=%fused_computation.13.clone.1 | convolution fusion | flops 70390016 | bytes 4734976 | tf_op jit(solution)/shard_map/while/body/eval_jaxpr/hts,thd->shd/dot_general | solution.py:60
  183.8 3.2 multiply_reduce_fusion.2
  191.6 19.4 %reshape.111 = f32[16,16,16,16,16]{2,1,4,3,0:T(8,128)} reshape(f32[16,256,256]{1,2,0:T(8,128)} %copy-done.2) | data formatting | bytes 8388608 | tf_op jit(solution)/shard_map/while/body/eval_jaxpr/reshape | solution.py:93
  211.0 30.4 %fusion.135 = f32[16,16,16,31,1]{3,1,4,2,0:T(8,128)S(1)} fusion(f32[16,16,16,16,16]{2,1,4,3,0:T(8,128)} %reshape.111, s32[16,16]{0,1:T(8,128)S(1)} %get-tuple-element.314), kind=kOutput, calls=%fused_computation.53.clone.1 | convolution fusion | flops 390086144 | bytes 4703232 | tf_op jit(solution)/shard_map/while/body/eval_jaxpr/haubv,uve->habe/dot_general | solution.py:91
  241.4 3.5 fusion.136
  245.8 2.4 copy.81
  248.2 9.7 %all-to-all-start.2 = ((bf16[2,128,2,512]{3,0,2,1:T(2,128)(2,1)}), bf16[2,128,2,512]{3,0,2,1:T(2,128)(2,1)S(1)}, u32[]{:S(2)}, u32[]{:S(2)}) async-start(bf16[2,128,2,512]{3,0,2,1:T(2,128)(2,1)} %bitcast.14), calls=%async_computation.2 | async-start | bytes 1048576 | tf_op jit(solution)/shard_map/all_to_all | solution.py:167
  259.0 59.0 %psum.14 = f32[16,31,31]{1,2,0:T(8,128)S(1)} all-reduce(f32[16,31,31]{1,2,0:T(8,128)S(1)} %reduce_sum.63), channel_id=1, replica_groups=mesh['ha'=16,'wa'=8] {'ha'}, use_global_device_ids=true, to_apply=%region_10.11 | all-reduce | flops 15376 | bytes 123008 | tf_op jit(solution)/shard_map/psum | solution.py:174
  318.0 44.4 %psum.15 = f32[16,31,31]{1,2,0:T(8,128)S(1)} all-reduce(f32[16,31,31]{1,2,0:T(8,128)S(1)} %psum.14), channel_id=1, replica_groups=mesh['ha'=16,'wa'=8] {'wa'}, use_global_device_ids=true, to_apply=%region_11.12 | all-reduce | flops 15376 | bytes 123008 | tf_op jit(solution)/shard_map/psum | solution.py:174
  (99 shorter events, 30.8 us)
Async XLA Ops:
  0.6 17.6 %copy-start = (f32[16,31,31]{2,0,1:T(8,128)S(1)}, f32[16,31,31]{2,0,1:T(8,128)}, u32[]{:S(2)}) copy-start(f32[16,31,31]{2,0,1:T(8,128)} %param.13) | copy-start | bytes 184516
  3.5 24.4 %all-to-all-start = ((bf16[2,128,2,512]{3,2,0,1:T(2,128)(2,1)}), bf16[2,128,2,512]{3,2,0,1:T(2,128)(2,1)S(1)}, u32[]{:S(2)}, u32[]{:S(2)}) async-start(bf16[2,128,2,512]{3,2,0,1:T(2,128)(2,1)} %bitcast.1), calls=%async_computation | async-start | bytes 1048576 | tf_op jit(solution)/shard_map/all_to_all | solution.py:140
  14.7 0.6 copy-start.11
  27.9 23.2 %copy-start.9 = (bf16[2,128,2,512]{3,2,0,1:T(2,128)(2,1)}, bf16[2,128,2,512]{3,2,0,1:T(2,128)(2,1)S(1)}, u32[]{:S(2)}) copy-start(bf16[2,128,2,512]{3,2,0,1:T(2,128)(2,1)S(1)} %all-to-all-done) | copy-start | bytes 1572868
  27.9 52.6 %all-to-all-start.1 = ((bf16[2,128,2,512]{3,2,0,1:T(2,128)(2,1)}), bf16[2,128,2,512]{3,2,0,1:T(2,128)(2,1)}, u32[]{:S(2)}, u32[]{:S(2)}) async-start(bf16[2,128,2,512]{3,2,0,1:T(2,128)(2,1)} %bitcast.12), calls=%async_computation.1 | async-start | bytes 1048576 | tf_op jit(solution)/shard_map/all_to_all | solution.py:149
  74.6 5.4 %copy-start.10 = (bf16[2,128,2,512]{3,2,0,1:T(2,128)(2,1)S(1)}, bf16[2,128,2,512]{3,2,0,1:T(2,128)(2,1)}, u32[]{:S(2)}) copy-start(bf16[2,128,2,512]{3,2,0,1:T(2,128)(2,1)} %copy-done.9) | copy-start | bytes 1572868
  80.0 3.0 copy-start.5
  80.0 3.0 copy-start.6
  80.0 3.0 copy-start.12
  80.1 3.0 copy-start.15
  94.2 3.2 copy-start.4
  94.2 3.2 copy-start.8
  102.5 3.4 copy-start.3
  106.7 1.9 copy-start.2
  106.7 1.9 copy-start.16
  129.8 30.4 %copy-start.13 = (f32[2,16,31,31]{2,3,1,0:T(8,128)S(1)}, f32[2,16,31,31]{2,3,1,0:T(8,128)}, u32[]{:S(2)}) copy-start(f32[2,16,31,31]{2,3,1,0:T(8,128)} %get-tuple-element.296) | copy-start | bytes 369028 | tf_op jit(solution)/shard_map/while
  129.8 34.7 %copy-start.7 = (bf16[512,512]{1,0:T(8,128)(2,1)S(1)}, bf16[512,512]{1,0:T(8,128)(2,1)}, u32[]{:S(2)}) copy-start(bf16[512,512]{1,0:T(8,128)(2,1)} %get-tuple-element.327) | copy-start | bytes 1572868 | tf_op jit(solution)/shard_map/while
  163.7 0.8 copy-start.14
  175.4 3.2 copy-start.4
  175.4 3.2 copy-start.8
  183.8 3.4 copy-start.3
  188.0 1.9 copy-start.2
  188.0 1.9 copy-start.16
  211.0 30.4 %copy-start.13 = (f32[2,16,31,31]{2,3,1,0:T(8,128)S(1)}, f32[2,16,31,31]{2,3,1,0:T(8,128)}, u32[]{:S(2)}) copy-start(f32[2,16,31,31]{2,3,1,0:T(8,128)} %get-tuple-element.296) | copy-start | bytes 369028 | tf_op jit(solution)/shard_map/while
  211.0 34.7 %copy-start.7 = (bf16[512,512]{1,0:T(8,128)(2,1)S(1)}, bf16[512,512]{1,0:T(8,128)(2,1)}, u32[]{:S(2)}) copy-start(bf16[512,512]{1,0:T(8,128)(2,1)} %get-tuple-element.327) | copy-start | bytes 1572868 | tf_op jit(solution)/shard_map/while
  244.9 0.8 copy-start.14
  245.8 118.9 %copy-start.1 = (f32[16,31,31]{2,0,1:T(8,128)S(1)}, f32[16,31,31]{2,0,1:T(8,128)}, u32[]{:S(2)}) copy-start(f32[16,31,31]{2,0,1:T(8,128)} %param.13) | copy-start | bytes 184516
  248.2 115.2 %all-to-all-start.2 = ((bf16[2,128,2,512]{3,0,2,1:T(2,128)(2,1)}), bf16[2,128,2,512]{3,0,2,1:T(2,128)(2,1)S(1)}, u32[]{:S(2)}, u32[]{:S(2)}) async-start(bf16[2,128,2,512]{3,0,2,1:T(2,128)(2,1)} %bitcast.14), calls=%async_computation.2 | async-start | bytes 1048576 | tf_op jit(solution)/shard_map/all_to_all | solution.py:167
